TPU v7x, 512 devices: a whole 4x4x16 slice. The times are simulated.
512 devices in a mesh: row: 8 (over y, core), col: 16 (over z), ch: 4 (over x).
Axes of the slice: x: 4, y: 4, z: 16, core: 2. Of those that a mesh axis runs over, the one named last changes fastest.
Arguments:
- image: bfloat16 [256, 32, 2048], P('ch', 'row', 'col'), may hold values from -6 to 6
- depth_kernel: float32 [256, 49], P('ch'), may hold values from -0.875 to 0.875
- norm_gain: float32 [256], P('ch'), may hold values from 0.25 to 1.75
- norm_shift: float32 [256], P('ch'), may hold values from -3 to 3
- expand_weight: bfloat16 [256, 1024], P(None, 'ch'), may hold values from -0.375 to 0.375
- expand_bias: float32 [1024], replicated, may hold values from -3 to 3
- reduce_weight: bfloat16 [1024, 256], P('ch'), may hold values from -0.1875 to 0.1875
- cotangent: bfloat16 [256, 32, 2048], P('ch', 'row', 'col'), may hold values from -6 to 6
Outputs:
- result: bfloat16 [256, 32, 2048], P('ch', 'row', 'col')
- grad_image: bfloat16 [256, 32, 2048], P('ch', 'row', 'col')
- grad_kernel: float32 [256, 49], P('ch')
- grad_gain: float32 [256], P('ch')
- grad_shift: float32 [256], P('ch')
- grad_expand: float32 [256, 1024], P(None, 'ch')
- grad_offset: float32 [1024], P('ch')
- grad_reduce: float32 [1024, 256], P('ch')
All inputs are finite; a program needn't handle non-finite values.
Results may differ from a plain program's by a relative error of at most 0.011.
Values may be sent and summed in bfloat16 or wider, within the bound.
No kernel may reach another device: no remote copies, remote signals or barrier semaphores. Data moves between devices by JAX's collectives and lax.ppermute only.
A program may use at most 64 MiB of HBM per device.

v0:
```python
import jax
import jax.numpy as jnp
from jax import lax
from jax.sharding import PartitionSpec as P

KSIZE = 7
epsilon = 1e-06
root_two_pi = 0.7978845608028654
cubic_coef = 0.044715


def padded_2(x, sides, width):
    for axis, dim in sides:
        size, length = (lax.axis_size(axis), x.shape[dim])
        up = [(i, (i + 1) % size) for i in range(size - 1)]
        down = [(j, i) for i, j in up]
        last = lax.slice_in_dim(x, length - width, length, axis=dim)
        leading = lax.slice_in_dim(x, 0, width, axis=dim)
        before = lax.ppermute(last, axis, up)
        after = lax.ppermute(leading, axis, down)
        x = jnp.concatenate([before, x, after], axis=dim)
    return x


def product(left, right, dims):
    return lax.dot_general(
        left.astype(jnp.float32),
        right.astype(jnp.float32),
        dims,
        preferred_element_type=jnp.float32,
    )


def gelu_pair(hidden):
    inner = root_two_pi * (hidden + cubic_coef * hidden * hidden * hidden)
    tangent = jnp.tanh(inner)
    value = 0.5 * hidden * (1.0 + tangent)
    slope = 0.5 * (1.0 + tangent) + 0.5 * hidden * (1.0 - tangent * tangent) * root_two_pi * (
        1.0 + 3.0 * cubic_coef * hidden * hidden
    )
    return (value, slope)


def tap_window(padded, kernel, tap, first, second, tile_rows, tile_cols):
    window = lax.dynamic_slice(
        padded, (jnp.int32(0), first, second), (padded.shape[0], tile_rows, tile_cols)
    )
    weight = lax.dynamic_slice_in_dim(kernel, tap, 1, 1)
    return weight[:, :, None] * window


def forward_taps(padded, kernel, span, tile_rows, tile_cols):

    def forward_step(tap, accum):
        tap = jnp.asarray(tap).astype(jnp.int32)
        first = tap // span
        second = tap % span
        return accum + tap_window(padded, kernel, tap, first, second, tile_rows, tile_cols)

    accum = jnp.zeros((padded.shape[0], tile_rows, tile_cols), jnp.float32)
    return lax.fori_loop(0, span * span, forward_step, accum)


def backward_taps(padded, kernel, span, tile_rows, tile_cols):
    reach = span - 1

    def backward_step(tap, accum):
        tap = jnp.asarray(tap).astype(jnp.int32)
        first = reach - tap // span
        second = reach - tap % span
        return accum + tap_window(padded, kernel, tap, first, second, tile_rows, tile_cols)

    accum = jnp.zeros((padded.shape[0], tile_rows, tile_cols), jnp.float32)
    return lax.fori_loop(0, span * span, backward_step, accum)


def kernel_grad(grad_mixed, padded, span, tile_rows, tile_cols):

    def kernel_step(tap, table):
        tap = jnp.asarray(tap).astype(jnp.int32)
        first = tap // span
        second = tap % span
        window = lax.dynamic_slice(
            padded, (jnp.int32(0), first, second), (padded.shape[0], tile_rows, tile_cols)
        )
        column = jnp.sum(grad_mixed * window, axis=(1, 2))
        return lax.dynamic_update_slice_in_dim(table, column[:, None], tap, 1)

    table = jnp.zeros((grad_mixed.shape[0], span * span), jnp.float32)
    return lax.fori_loop(0, span * span, kernel_step, table)


def body(
    image, depth_kernel, norm_gain, norm_shift, expand_weight, expand_bias, reduce_weight, cotangent
):
    channels, tile_rows, tile_cols = image.shape
    pixels = tile_rows * tile_cols
    all_channels = channels * lax.axis_size("ch")
    hid_local = reduce_weight.shape[0]
    half = KSIZE // 2
    padded = padded_2(image, (("row", 1), ("col", 2)), half).astype(jnp.float32)
    mixed = forward_taps(padded, depth_kernel, KSIZE, tile_rows, tile_cols)
    flat_cot = cotangent.reshape(channels, pixels)
    contract_first = (((0,), (0,)), ((), ()))
    contract_last = (((1,), (1,)), ((), ()))
    plain = (((1,), (0,)), ((), ()))
    centre = lax.psum(jnp.sum(mixed, axis=0), "ch") / all_channels
    diff = mixed - centre
    variance = lax.psum(jnp.sum(diff * diff, axis=0), "ch") / all_channels
    inverse = lax.rsqrt(variance + epsilon)
    normed = diff * inverse
    normal = (normed * norm_gain[:, None, None] + norm_shift[:, None, None]).astype(jnp.bfloat16)
    flat_normal = normal.reshape(channels, pixels)
    bias_local = lax.dynamic_slice_in_dim(expand_bias, lax.axis_index("ch") * hid_local, hid_local)
    full_normal = lax.all_gather(flat_normal, "ch", axis=0, tiled=True)
    hidden = product(expand_weight, full_normal, contract_first) + bias_local[:, None]
    value, slope = gelu_pair(hidden)
    active = value.astype(jnp.bfloat16)
    mlp_local = lax.psum_scatter(
        product(reduce_weight, active, contract_first), "ch", scatter_dimension=0, tiled=True
    )
    full_cot = lax.all_gather(flat_cot, "ch", axis=0, tiled=True)
    grad_act = product(reduce_weight, full_cot, plain)
    grad_hidden = (grad_act * slope).astype(jnp.bfloat16)
    grad_red = product(active, full_cot, contract_last)
    grad_exp = product(full_normal, grad_hidden, contract_last)
    grad_off = jnp.sum(grad_hidden.astype(jnp.float32), axis=1)
    grad_local = lax.psum_scatter(
        product(expand_weight, grad_hidden, plain).astype(jnp.bfloat16),
        "ch",
        scatter_dimension=0,
        tiled=True,
    ).astype(jnp.float32)
    grad_normal = grad_local.reshape(channels, tile_rows, tile_cols)
    grad_normed = grad_normal * norm_gain[:, None, None]
    plain_sum, cross_sum = lax.psum(
        (jnp.sum(grad_normed, axis=0), jnp.sum(grad_normed * normed, axis=0)), "ch"
    )
    grad_gain = jnp.sum(grad_normal * normed, axis=(1, 2))
    grad_shift = jnp.sum(grad_normal, axis=(1, 2))
    grad_mixed = inverse * (
        grad_normed - plain_sum / all_channels - normed * (cross_sum / all_channels)
    )
    result = (image.astype(jnp.float32) + mlp_local.reshape(channels, tile_rows, tile_cols)).astype(
        jnp.bfloat16
    )
    grad_pad = padded_2(grad_mixed.astype(jnp.bfloat16), (("row", 1), ("col", 2)), half).astype(
        grad_mixed.dtype
    )
    grad_image = (
        cotangent.astype(jnp.float32)
        + backward_taps(grad_pad, depth_kernel, KSIZE, tile_rows, tile_cols)
    ).astype(jnp.bfloat16)
    grad_kernel = kernel_grad(grad_mixed, padded, KSIZE, tile_rows, tile_cols)
    totals = lax.psum(
        (grad_kernel, grad_gain, grad_shift, grad_exp, grad_off, grad_red), ("row", "col")
    )
    pixels_all = pixels * lax.axis_size("row") * lax.axis_size("col")
    scale = float(pixels_all) ** (-0.5)
    return (
        result,
        grad_image,
        totals[0] * scale,
        totals[1] * scale,
        totals[2] * scale,
        totals[3] * scale,
        totals[4] * scale,
        totals[5] * scale,
    )


def solution(mesh):
    in_specs = (
        P("ch", "row", "col"),
        P("ch", None),
        P("ch"),
        P("ch"),
        P(None, "ch"),
        P(),
        P("ch", None),
        P("ch", "row", "col"),
    )
    out_specs = (
        P("ch", "row", "col"),
        P("ch", "row", "col"),
        P("ch", None),
        P("ch"),
        P("ch"),
        P(None, "ch"),
        P("ch"),
        P("ch", None),
    )
    return jax.shard_map(body, mesh=mesh, in_specs=in_specs, out_specs=out_specs, check_vma=False)
```

profile of v0, /device:TPU:1, one launch (start us, length us, event | category | flops | bytes accessed | tf_op | source)
XLA Modules:
  0.0 1113.7 jit_solution(2712978404241594079)
XLA Ops:
  8.1 1.0 fusion.13
  9.0 4.6 collective-permute-start
  13.6 5.5 collective-permute-start.1
  20.3 2.8 collective-permute-start.2
  23.1 1.3 collective-permute-start.3
  24.4 10.6 all_gather.7
  36.5 57.9 %while.48 = (s32[]{:T(128)}, f32[64,4,128]{2,1,0:T(4,128)S(1)}, f32[64,49]{0,1:T(8,128)}, f32[64,10,134]{2,1,0:T(8,128)S(1)}, s32[]{:T(128)}, /*index=5*/s32[]{:T(128)}, s32[]{:T(128)}, s32[]{:T(128)}, s32[]{:T(128)}, s32[]{:T(128)}) while((s32[]{:T(128)}, f32[64,4,128]{2,1,0:T(4,128)S(1)}, f32[64,49]{0,1:T(8,128)}, ...), condition=%wide.region_1.2_spmd.clone, body=%wide.region_0.1_spmd.clone.sunk | while | flops 98325 | bytes 394290 | solution.py:61
  94.4 7.8 psum.70
  102.4 6.0 psum.71
  109.3 10.1 all_gather.6
  119.6 1.1 fusion.8
  123.7 1.0 copy.25
  124.7 346.0 %all-reduce.5.cloned.1.call-done = (f32[256,256]{1,0:T(8,128)}, f32[256,256]{1,0:T(8,128)}) async-done(((f32[256,256]{1,0:T(8,128)}, f32[256,256]{1,0:T(8,128)}), (f32[256,256]{1,0:T(8,128)}, f32[256,256]{1,0:T(8,128)})) %all-reduce.5.cloned.1.call-update) | async-done | bytes 524304 | tf_op jit(solution)/shard_map/psum | solution.py:155
  470.8 1.9 broadcast_multiply_fusion
  472.6 1.0 copy.28
  474.4 8.4 all-reduce.2
  482.9 50.7 %while.47 = (s32[]{:T(128)}, f32[64,49]{0,1:T(8,128)S(1)}, f32[64,10,134]{2,1,0:T(8,128)S(1)}, f32[64,4,128]{2,1,0:T(4,128)S(1)}, s32[]{:T(128)}, /*index=5*/s32...) while((s32[]{:T(128)}, f32[64,49]{0,1:T(8,128)S(1)}, f32[64,10,134]{2,1,0:T(8,128)S(1)}, ...), condition=%wide.region_16.17_spmd, body=%wide.region_14.16_spmd.sunk | while | flops 65492 | bytes 263208 | solution.py:90
  483.0 0.9 multiply_reduce_fusion.6
  484.0 0.9 multiply_reduce_fusion.6
  485.1 0.9 multiply_reduce_fusion.6
  489.2 0.9 multiply_reduce_fusion.6
  490.2 0.9 multiply_reduce_fusion.6
  491.3 0.9 multiply_reduce_fusion.6
  533.7 477.5 %all-reduce = (f32[64,49]{0,1:T(8,128)S(1)}, f32[64]{0:T(128)S(1)}, f32[64]{0:T(128)S(1)}, f32[256]{0:T(256)S(1)}) all-reduce(f32[64,49]{0,1:T(8,128)S(1)} %get-tuple-element.351, f32[64]{0:T(128)S(1)} %get-tuple-element.382, f32[64]{0:T(128)S(1)} %get-tuple-element.384, ...), channel_id=1, replica_groups=mesh['row'=8,'col'=16,'ch'=4] {'row','col'}, use_global_device_ids=true, to_apply=%region_17.18 | all-reduce | flops 3520 | bytes 28160 | tf_op jit(solution)/shard_map/psum | solution.py:155
  1012.4 1.9 collective-permute-start.4
  1014.3 19.1 %collective-permute-start.5 = (bf16[64,3,128]{2,1,0:T(4,128)(2,1)S(1)}, bf16[64,3,128]{2,1,0:T(4,128)(2,1)S(1)}, u32[]{:S(2)}, u32[]{:S(2)}) collective-permute-start(bf16[64,3,128]{2,1,0:T(4,128)(2,1)S(1)} %get-tuple-element.425), channel_id=1, source_target_pairs={{64,0},{128,64},{192,128},{256,192},{320,256},{384,320},{448,384},... | collective-permute-start | bytes 147464 | tf_op jit(solution)/shard_map/ppermute | solution.py:20
  1034.6 1.3 collective-permute-start.6
  1035.9 1.3 collective-permute-start.7
  1037.7 3.5 collective-permute-done.6
  1041.2 3.8 collective-permute-done.7
  1045.8 57.9 %while.49 = (s32[]{:T(128)}, f32[64,4,128]{2,1,0:T(4,128)S(1)}, f32[64,49]{0,1:T(8,128)}, f32[64,10,134]{2,1,0:T(8,128)S(1)}, s32[]{:T(128)}, /*index=5*/s32[]{:...) while((s32[]{:T(128)}, f32[64,4,128]{2,1,0:T(4,128)S(1)}, ...), condition=%wide.region_13.14_spmd.clone, body=%wide.region_12.13_spmd.clone.sunk | while | flops 98327 | bytes 394322 | solution.py:74
  1104.4 1.0 copy.26
  (350 shorter events, 165.8 us)
Async XLA Ops:
  8.0 112.7 %copy-start = (bf16[256,256]{1,0:T(8,128)(2,1)S(1)}, bf16[256,256]{1,0:T(8,128)(2,1)}, u32[]{:S(2)}) copy-start(bf16[256,256]{1,0:T(8,128)(2,1)} %param.20) | copy-start | bytes 393220
  8.0 11.1 copy-start.3
  8.0 462.7 %all-reduce.5.cloned.1.call-start = ((), (), s32[]{:S(2)}) async-start(), calls=%async_computation.4 | async-start | bytes 1048576 | tf_op jit(solution)/shard_map/psum | solution.py:155
  9.0 10.1 collective-permute-start
  13.6 6.3 collective-permute-start.1
  19.1 0.9 copy-start.1
  20.3 15.5 %collective-permute-start.2 = (bf16[64,10,3]{2,1,0:T(8,128)(2,1)S(1)}, bf16[64,10,3]{2,1,0:T(8,128)(2,1)S(1)}, u32[]{:S(2)}, u32[]{:S(2)}) collective-permute-start(bf16[64,10,3]{2,1,0:T(8,128)(2,1)S(1)} %get-tuple-element.422), channel_id=1, source_target_pairs={{0,4},{4,8},{8,12},{12,16},{16,20},{20,24},{24,28},{28,32},{32,36}... | collective-permute-start | bytes 11528 | tf_op jit(solution)/shard_map/ppermute | solution.py:19
  23.1 12.7 %collective-permute-start.3 = (bf16[64,10,3]{2,1,0:T(8,128)(2,1)S(1)}, bf16[64,10,3]{2,1,0:T(8,128)(2,1)S(1)}, u32[]{:S(2)}, u32[]{:S(2)}) collective-permute-start(bf16[64,10,3]{2,1,0:T(8,128)(2,1)S(1)} %get-tuple-element.423), channel_id=1, source_target_pairs={{4,0},{8,4},{12,8},{16,12},{20,16},{24,20},{28,24},{32,28},{36,32}... | collective-permute-start | bytes 11528 | tf_op jit(solution)/shard_map/ppermute | solution.py:20
  108.4 0.7 copy-start.4
  108.4 0.7 copy-start.5
  109.3 10.1 copy-start.2
  122.1 350.5 %reduce-scatter.9.cloned.1.call-start = ((), (), s32[]{:S(2)}) async-start(), calls=%async_computation.3 | async-start | bytes 327680
  123.3 981.1 %reduce-scatter.7.cloned.1.call-start = ((), (), s32[]{:S(2)}) async-start(), calls=%async_computation.2 | async-start | bytes 655360
  1012.4 21.6 %collective-permute-start.4 = (bf16[64,3,128]{2,1,0:T(4,128)(2,1)S(1)}, bf16[64,3,128]{2,1,0:T(4,128)(2,1)S(1)}, u32[]{:S(2)}, u32[]{:S(2)}) collective-permute-start(bf16[64,3,128]{2,1,0:T(4,128)(2,1)S(1)} %get-tuple-element.424), channel_id=1, source_target_pairs={{0,64},{64,128},{128,192},{192,256},{256,320},{320,384},{384,448},... | collective-permute-start | bytes 147464 | tf_op jit(solution)/shard_map/ppermute | solution.py:19
  1014.3 20.0 %collective-permute-start.5 = (bf16[64,3,128]{2,1,0:T(4,128)(2,1)S(1)}, bf16[64,3,128]{2,1,0:T(4,128)(2,1)S(1)}, u32[]{:S(2)}, u32[]{:S(2)}) collective-permute-start(bf16[64,3,128]{2,1,0:T(4,128)(2,1)S(1)} %get-tuple-element.425), channel_id=1, source_target_pairs={{64,0},{128,64},{192,128},{256,192},{320,256},{384,320},{448,384},... | collective-permute-start | bytes 147464 | tf_op jit(solution)/shard_map/ppermute | solution.py:20
  1034.6 6.7 collective-permute-start.6
  1035.9 9.2 collective-permute-start.7
Sparse Core Ops, SparseCore 0:
  122.3 348.4 all-reduce.4
Sparse Core Ops, SparseCore 1:
  125.4 38.8 reduce-scatter.8
  167.0 28.9 reduce-scatter.6
where the time goes:
time: 1120 us; the launch traced here: 1110 us
  blocking collectives  520 us (46%)
  waiting for transfers between devices  355 us (32%)
  other arithmetic  97.2 us (9%)
  local copies, waits for them, and re-layouts  76.4 us (7%)
  starting transfers between devices  37.9 us (3%)
  between operations  15.7 us (1%)
    psum x1, blocking collectives, body(): lax.psum((grad_kernel, grad_gain, grad_shift, grad_exp, grad_off, grad_re...  477 us
    psum x1, waiting for transfers between devices, body(): lax.psum((grad_kernel, grad_gain, grad_shift, grad_exp, grad_off, grad_re...  346 us
    mul x98, local copies, waits for them, and re-layouts, tap_window(): return weight[:, :, None] * window  68.2 us
    reduce_sum x49, other arithmetic, kernel_step(): column = jnp.sum(grad_mixed * window, axis=(1, 2))  46.4 us
    ppermute x4, starting transfers between devices, padded_2(): after = lax.ppermute(leading, axis, down)  27.1 us
  transfers between devices with their start and end apart: 11, of which 5 were waited for; matrix products, arithmetic and copies ran while one was open for 10% of the time, Pallas kernels for 0%

commit v1 on v0

--- a/solution.py
+++ b/solution.py
@@ -152,9 +152,9 @@
         + backward_taps(grad_pad, depth_kernel, KSIZE, tile_rows, tile_cols)
     ).astype(jnp.bfloat16)
     grad_kernel = kernel_grad(grad_mixed, padded, KSIZE, tile_rows, tile_cols)
-    totals = lax.psum(
-        (grad_kernel, grad_gain, grad_shift, grad_exp, grad_off, grad_red), ("row", "col")
-    )
+    totals = (grad_kernel, grad_gain, grad_shift, grad_exp, grad_off, grad_red)
+    for over in ("row", "col"):
+        totals = lax.psum(totals, over)
     pixels_all = pixels * lax.axis_size("row") * lax.axis_size("col")
     scale = float(pixels_all) ** (-0.5)
     return (

time: 1120 us -> 451 us (0.40)
  blocking collectives: 520 us -> 115 us
  waiting for transfers between devices: 355 us -> 96.9 us
    psum x1 -> x2, blocking collectives: 477 us -> 72.8 us  [body(): totals = lax.psum(totals, over)]
    psum x1 -> x2, waiting for transfers between devices: 346 us -> 86.5 us  [body(): totals = lax.psum(totals, over)]
    ppermute x4, starting transfers between devices: 27.1 us -> 11.3 us  [padded_2(): after = lax.ppermute(leading, axis, down)]
    ppermute x4, starting transfers between devices: 10.6 us -> 21.9 us  [padded_2(): before = lax.ppermute(last, axis, up)]
  transfers between devices with their start and end apart: 11 -> 12, of which waited for: 5 -> 5; matrix products, arithmetic and copies ran while one was open for 10% -> 26% of each run, Pallas kernels for 0% -> 0%
where the time goes in v1:
time: 451 us; the launch traced here: 446 us
  blocking collectives  115 us (25%)
  other arithmetic  97.2 us (22%)
  waiting for transfers between devices  96.9 us (21%)
  local copies, waits for them, and re-layouts  76.4 us (17%)
  starting transfers between devices  33.3 us (7%)
  between operations  15.8 us (4%)
  loops' own time  8.1 us (2%)
    psum x2, waiting for transfers between devices, body(): totals = lax.psum(totals, over)  86.5 us
    psum x2, blocking collectives, body(): totals = lax.psum(totals, over)  72.8 us
    mul x98, local copies, waits for them, and re-layouts, tap_window(): return weight[:, :, None] * window  68.2 us
    reduce_sum x49, other arithmetic, kernel_step(): column = jnp.sum(grad_mixed * window, axis=(1, 2))  46.4 us
    ppermute x4, starting transfers between devices, padded_2(): before = lax.ppermute(last, axis, up)  21.9 us
    add x49, other arithmetic, forward_step(): accum + tap_window(padded, kernel, tap, first, second, tile_rows, tile_cols)  21.2 us
    add x49, other arithmetic, backward_step(): accum + tap_window(padded, kernel, tap, first, second, tile_rows, tile_cols)  21.2 us
    ppermute x4, starting transfers between devices, padded_2(): after = lax.ppermute(leading, axis, down)  11.3 us
  transfers between devices with their start and end apart: 12, of which 5 were waited for; matrix products, arithmetic and copies ran while one was open for 26% of the time, Pallas kernels for 0%

profile of v1, /device:TPU:1, one launch (start us, length us, event | category | flops | bytes accessed | tf_op | source)
XLA Modules:
  0.0 446.1 jit_solution(630205602618956242)
XLA Ops:
  8.1 1.0 fusion.13
  9.0 4.6 %collective-permute-start = (bf16[64,3,128]{2,1,0:T(4,128)(2,1)S(1)}, bf16[64,3,128]{2,1,0:T(4,128)(2,1)S(1)}, u32[]{:S(2)}, u32[]{:S(2)}) collective-permute-start(bf16[64,3,128]{2,1,0:T(4,128)(2,1)S(1)} %get-tuple-element.432), channel_id=1, source_target_pairs={{0,64},{64,128},{128,192},{192,256},{256,320},{320,384},{384,448},... | collective-permute-start | bytes 147464 | tf_op jit(solution)/shard_map/ppermute | solution.py:19
  13.6 5.5 %collective-permute-start.1 = (bf16[64,3,128]{2,1,0:T(4,128)(2,1)S(1)}, bf16[64,3,128]{2,1,0:T(4,128)(2,1)S(1)}, u32[]{:S(2)}, u32[]{:S(2)}) collective-permute-start(bf16[64,3,128]{2,1,0:T(4,128)(2,1)S(1)} %get-tuple-element.433), channel_id=1, source_target_pairs={{64,0},{128,64},{192,128},{256,192},{320,256},{384,320},{448,384},... | collective-permute-start | bytes 147464 | tf_op jit(solution)/shard_map/ppermute | solution.py:20
  20.3 2.8 collective-permute-start.2
  23.1 1.3 collective-permute-start.3
  24.4 10.6 %all_gather.7 = bf16[256,512]{1,0:T(8,128)(2,1)S(1)} all-gather(bf16[64,512]{1,0:T(8,128)(2,1)S(1)} %bitcast.43), channel_id=1, replica_groups=mesh['row'=8,'col'=16,'ch'=4] {'ch'}, dimensions={0}, use_global_device_ids=true | all-gather | bytes 327680 | tf_op jit(solution)/shard_map/all_gather | solution.py:122
  36.5 57.9 %while.48 = (s32[]{:T(128)}, f32[64,4,128]{2,1,0:T(4,128)S(1)}, f32[64,49]{0,1:T(8,128)}, f32[64,10,134]{2,1,0:T(8,128)S(1)}, s32[]{:T(128)}, /*index=5*/s32[]{:T(128)}, s32[]{:T(128)}, s32[]{:T(128)}, s32[]{:T(128)}, s32[]{:T(128)}) while((s32[]{:T(128)}, f32[64,4,128]{2,1,0:T(4,128)S(1)}, f32[64,49]{0,1:T(8,128)}, ...), condition=%wide.region_1.2_spmd.clone, body=%wide.region_0.1_spmd.clone.sunk | while | flops 98325 | bytes 394290 | solution.py:61
  94.4 7.8 %psum.112 = f32[4,128]{1,0:T(4,128)S(1)} all-reduce(f32[4,128]{1,0:T(4,128)S(1)} %reduce_sum.81), channel_id=1, replica_groups=mesh['row'=8,'col'=16,'ch'=4] {'ch'}, use_global_device_ids=true, to_apply=%region_3.4 | all-reduce | flops 512 | bytes 4096 | tf_op jit(solution)/shard_map/psum | solution.py:107
  102.4 6.0 %psum.113 = f32[4,128]{1,0:T(4,128)S(1)} all-reduce(f32[4,128]{1,0:T(4,128)S(1)} %multiply_reduce_fusion.4), channel_id=1, replica_groups=mesh['row'=8,'col'=16,'ch'=4] {'ch'}, use_global_device_ids=true, to_apply=%region_5.6 | all-reduce | flops 512 | bytes 4096 | tf_op jit(solution)/shard_map/psum | solution.py:109
  109.3 10.1 %all_gather.6 = bf16[256,512]{1,0:T(8,128)(2,1)S(1)} all-gather(bf16[64,512]{1,0:T(8,128)(2,1)S(1)} %bitcast.44), channel_id=1, replica_groups=mesh['row'=8,'col'=16,'ch'=4] {'ch'}, dimensions={0}, use_global_device_ids=true | all-gather | bytes 327680 | tf_op jit(solution)/shard_map/all_gather | solution.py:115
  119.6 1.1 fusion.8
  123.4 86.5 %all-reduce.10.cloned.1.call-done = (f32[256,256]{1,0:T(8,128)}, f32[256,256]{1,0:T(8,128)}) async-done(((f32[256,256]{1,0:T(8,128)}, f32[256,256]{1,0:T(8,128)}), (f32[256,256]{1,0:T(8,128)}, f32[256,256]{1,0:T(8,128)})) %all-reduce.10.cloned.1.call-update) | async-done | bytes 524304 | tf_op jit(solution)/shard_map/psum | solution.py:157
  210.3 1.0 copy.25
  211.4 1.0 copy.28
  213.1 7.8 %all-reduce.4 = (f32[4,128]{1,0:T(4,128)S(1)}, f32[4,128]{1,0:T(4,128)S(1)}) all-reduce(f32[4,128]{1,0:T(4,128)S(1)} %get-tuple-element.383, f32[4,128]{1,0:T(4,128)S(1)} %bitcast.48), channel_id=1, replica_groups=mesh['row'=8,'col'=16,'ch'=4] {'ch'}, use_global_device_ids=true, to_apply=%region_11.12 | all-reduce | flops 1024 | bytes 8192 | tf_op jit(solution)/shard_map/psum | solution.py:136
  221.1 50.7 %while.47 = (s32[]{:T(128)}, f32[64,49]{0,1:T(8,128)S(1)}, f32[64,10,134]{2,1,0:T(8,128)S(1)}, f32[64,4,128]{2,1,0:T(4,128)S(1)}, s32[]{:T(128)}, /*index=5*/s32...) while((s32[]{:T(128)}, f32[64,49]{0,1:T(8,128)S(1)}, f32[64,10,134]{2,1,0:T(8,128)S(1)}, ...), condition=%wide.region_16.17_spmd, body=%wide.region_14.16_spmd.sunk | while | flops 65492 | bytes 263208 | solution.py:90
  221.1 0.9 multiply_reduce_fusion.6
  222.2 0.9 multiply_reduce_fusion.6
  223.2 0.9 multiply_reduce_fusion.6
  227.3 0.9 multiply_reduce_fusion.6
  271.8 24.9 %all-reduce.2 = (f32[64,49]{0,1:T(8,128)S(1)}, f32[64]{0:T(128)S(1)}, f32[64]{0:T(128)S(1)}, f32[256]{0:T(256)S(1)}) all-reduce(f32[64,49]{0,1:T(8,128)S(1)} %get-tuple-element.351, f32[64]{0:T(128)S(1)} %get-tuple-element.382, f32[64]{0:T(128)S(1)} %get-tuple-element.384, ...), channel_id=1, replica_groups=mesh['row'=8,'col'=16,'ch'=4] {'row'}, use_global_device_ids=true, to_apply=%region_17.18 | all-reduce | flops 3520 | bytes 28160 | tf_op jit(solution)/shard_map/psum | solution.py:157
  296.7 47.9 %all-reduce = (f32[64,49]{0,1:T(8,128)S(1)}, f32[64]{0:T(128)S(1)}, f32[64]{0:T(128)S(1)}, f32[256]{0:T(256)S(1)}) all-reduce(f32[64,49]{0,1:T(8,128)S(1)} %get-tuple-element.416, f32[64]{0:T(128)S(1)} %get-tuple-element.417, f32[64]{0:T(128)S(1)} %get-tuple-element.418, ...), channel_id=1, replica_groups=mesh['row'=8,'col'=16,'ch'=4] {'col'}, use_global_device_ids=true, to_apply=%region_18.19 | all-reduce | flops 3520 | bytes 28160 | tf_op jit(solution)/shard_map/psum | solution.py:157
  345.8 12.7 %collective-permute-start.4 = (bf16[64,3,128]{2,1,0:T(4,128)(2,1)S(1)}, bf16[64,3,128]{2,1,0:T(4,128)(2,1)S(1)}, u32[]{:S(2)}, u32[]{:S(2)}) collective-permute-start(bf16[64,3,128]{2,1,0:T(4,128)(2,1)S(1)} %get-tuple-element.430), channel_id=1, source_target_pairs={{0,64},{64,128},{128,192},{192,256},{256,320},{320,384},{384,448},... | collective-permute-start | bytes 147464 | tf_op jit(solution)/shard_map/ppermute | solution.py:19
  358.5 3.2 collective-permute-start.5
  362.3 1.8 collective-permute-done.5
  364.4 1.8 collective-permute-start.6
  366.2 1.3 collective-permute-start.7
  368.0 3.5 collective-permute-done.6
  371.5 4.1 collective-permute-done.7
  376.4 57.9 %while.49 = (s32[]{:T(128)}, f32[64,4,128]{2,1,0:T(4,128)S(1)}, f32[64,49]{0,1:T(8,128)}, f32[64,10,134]{2,1,0:T(8,128)S(1)}, s32[]{:T(128)}, /*index=5*/s32[]{:...) while((s32[]{:T(128)}, f32[64,4,128]{2,1,0:T(4,128)S(1)}, ...), condition=%wide.region_13.14_spmd.clone, body=%wide.region_12.13_spmd.clone.sunk | while | flops 98327 | bytes 394322 | solution.py:74
  435.0 1.9 broadcast_multiply_fusion
  436.8 1.0 copy.26
  (354 shorter events, 167.4 us)
Async XLA Ops:
  8.0 112.7 %copy-start = (bf16[256,256]{1,0:T(8,128)(2,1)S(1)}, bf16[256,256]{1,0:T(8,128)(2,1)}, u32[]{:S(2)}) copy-start(bf16[256,256]{1,0:T(8,128)(2,1)} %param.20) | copy-start | bytes 393220
  8.0 11.1 %copy-start.3 = (bf16[64,4,128]{2,1,0:T(4,128)(2,1)S(1)}, bf16[64,4,128]{2,1,0:T(4,128)(2,1)}, u32[]{:S(2)}) copy-start(bf16[64,4,128]{2,1,0:T(4,128)(2,1)} %param.21) | copy-start | bytes 196612
  8.0 201.9 %all-reduce.10.cloned.1.call-start = ((), (), s32[]{:S(2)}) async-start(), calls=%async_computation.5 | async-start | bytes 1048576 | tf_op jit(solution)/shard_map/psum | solution.py:157
  9.0 10.1 %collective-permute-start = (bf16[64,3,128]{2,1,0:T(4,128)(2,1)S(1)}, bf16[64,3,128]{2,1,0:T(4,128)(2,1)S(1)}, u32[]{:S(2)}, u32[]{:S(2)}) collective-permute-start(bf16[64,3,128]{2,1,0:T(4,128)(2,1)S(1)} %get-tuple-element.432), channel_id=1, source_target_pairs={{0,64},{64,128},{128,192},{192,256},{256,320},{320,384},{384,448},... | collective-permute-start | bytes 147464 | tf_op jit(solution)/shard_map/ppermute | solution.py:19
  13.6 6.3 %collective-permute-start.1 = (bf16[64,3,128]{2,1,0:T(4,128)(2,1)S(1)}, bf16[64,3,128]{2,1,0:T(4,128)(2,1)S(1)}, u32[]{:S(2)}, u32[]{:S(2)}) collective-permute-start(bf16[64,3,128]{2,1,0:T(4,128)(2,1)S(1)} %get-tuple-element.433), channel_id=1, source_target_pairs={{64,0},{128,64},{192,128},{256,192},{320,256},{384,320},{448,384},... | collective-permute-start | bytes 147464 | tf_op jit(solution)/shard_map/ppermute | solution.py:20
  19.1 0.9 copy-start.1
  20.3 15.5 %collective-permute-start.2 = (bf16[64,10,3]{2,1,0:T(8,128)(2,1)S(1)}, bf16[64,10,3]{2,1,0:T(8,128)(2,1)S(1)}, u32[]{:S(2)}, u32[]{:S(2)}) collective-permute-start(bf16[64,10,3]{2,1,0:T(8,128)(2,1)S(1)} %get-tuple-element.428), channel_id=1, source_target_pairs={{0,4},{4,8},{8,12},{12,16},{16,20},{20,24},{24,28},{28,32},{32,36}... | collective-permute-start | bytes 11528 | tf_op jit(solution)/shard_map/ppermute | solution.py:19
  23.1 12.7 %collective-permute-start.3 = (bf16[64,10,3]{2,1,0:T(8,128)(2,1)S(1)}, bf16[64,10,3]{2,1,0:T(8,128)(2,1)S(1)}, u32[]{:S(2)}, u32[]{:S(2)}) collective-permute-start(bf16[64,10,3]{2,1,0:T(8,128)(2,1)S(1)} %get-tuple-element.429), channel_id=1, source_target_pairs={{4,0},{8,4},{12,8},{16,12},{20,16},{24,20},{28,24},{32,28},{36,32}... | collective-permute-start | bytes 11528 | tf_op jit(solution)/shard_map/ppermute | solution.py:20
  108.4 0.7 copy-start.4
  108.4 0.7 copy-start.5
  109.3 10.1 %copy-start.2 = (bf16[256,256]{1,0:T(8,128)(2,1)S(1)}, bf16[256,256]{1,0:T(8,128)(2,1)}, u32[]{:S(2)}) copy-start(bf16[256,256]{1,0:T(8,128)(2,1)} %param.18) | copy-start | bytes 393220
  122.1 89.2 %reduce-scatter.9.cloned.1.call-start = ((), (), s32[]{:S(2)}) async-start(), calls=%async_computation.3 | async-start | bytes 327680
  123.3 311.6 %all-reduce.8.cloned.1.call-start = ((), (), s32[]{:S(2)}) async-start(), calls=%async_computation.4 | async-start | bytes 1048576 | tf_op jit(solution)/shard_map/psum | solution.py:157
  209.9 226.9 %reduce-scatter.7.cloned.1.call-start = ((), (), s32[]{:S(2)}) async-start(), calls=%async_computation.2 | async-start | bytes 655360
  345.8 16.5 %collective-permute-start.4 = (bf16[64,3,128]{2,1,0:T(4,128)(2,1)S(1)}, bf16[64,3,128]{2,1,0:T(4,128)(2,1)S(1)}, u32[]{:S(2)}, u32[]{:S(2)}) collective-permute-start(bf16[64,3,128]{2,1,0:T(4,128)(2,1)S(1)} %get-tuple-element.430), channel_id=1, source_target_pairs={{0,64},{64,128},{128,192},{192,256},{256,320},{320,384},{384,448},... | collective-permute-start | bytes 147464 | tf_op jit(solution)/shard_map/ppermute | solution.py:19
  358.5 5.6 %collective-permute-start.5 = (bf16[64,3,128]{2,1,0:T(4,128)(2,1)S(1)}, bf16[64,3,128]{2,1,0:T(4,128)(2,1)S(1)}, u32[]{:S(2)}, u32[]{:S(2)}) collective-permute-start(bf16[64,3,128]{2,1,0:T(4,128)(2,1)S(1)} %get-tuple-element.431), channel_id=1, source_target_pairs={{64,0},{128,64},{192,128},{256,192},{320,256},{384,320},{448,384},... | collective-permute-start | bytes 147464 | tf_op jit(solution)/shard_map/ppermute | solution.py:20
  364.4 7.1 %collective-permute-start.6 = (bf16[64,10,3]{2,1,0:T(8,128)(2,1)S(1)}, bf16[64,10,3]{2,1,0:T(8,128)(2,1)S(1)}, u32[]{:S(2)}, u32[]{:S(2)}) collective-permute-start(bf16[64,10,3]{2,1,0:T(8,128)(2,1)S(1)} %get-tuple-element.426), channel_id=1, source_target_pairs={{0,4},{4,8},{8,12},{12,16},{16,20},{20,24},{24,28},{28,32},{32,36}... | collective-permute-start | bytes 11528 | tf_op jit(solution)/shard_map/ppermute | solution.py:19
  366.2 9.4 %collective-permute-start.7 = (bf16[64,10,3]{2,1,0:T(8,128)(2,1)S(1)}, bf16[64,10,3]{2,1,0:T(8,128)(2,1)S(1)}, u32[]{:S(2)}, u32[]{:S(2)}) collective-permute-start(bf16[64,10,3]{2,1,0:T(8,128)(2,1)S(1)} %get-tuple-element.427), channel_id=1, source_target_pairs={{4,0},{8,4},{12,8},{16,12},{20,16},{24,20},{28,24},{32,28},{36,32}... | collective-permute-start | bytes 11528 | tf_op jit(solution)/shard_map/ppermute | solution.py:20
Sparse Core Ops, SparseCore 0:
  122.3 87.5 all-reduce.9
  212.3 129.1 all-reduce.7
Sparse Core Ops, SparseCore 1:
  126.0 39.0 reduce-scatter.8
  213.2 27.6 reduce-scatter.6
